TPU v7x, 768 devices: a whole 4x8x12 slice. The times are simulated.
768 devices in a mesh: ctx: 48 (over z, y_lo), head: 16 (over y_hi, x, core).
Axes of the slice: x: 4, y: 8 (y_hi: 2, y_lo: 4; y = y_hi * 4 + y_lo), z: 12, core: 2. Of those that a mesh axis runs over, the one named last changes fastest.
Arguments:
- queries: bfloat16 [12288, 4096], P('ctx', 'head'), may hold values from -48 to 48
- enc_keys: bfloat16 [1536, 4096], P('ctx', 'head'), may hold values from -4 to 4
- enc_values: bfloat16 [1536, 4096], P('ctx', 'head'), may hold values from -6 to 6
- grad_out: bfloat16 [12288, 4096], P('ctx', 'head'), may hold values from -48 to 48
- out_weight: bfloat16 [4096, 4096], P('head'), may hold values from -0.09375 to 0.09375
Outputs:
- query_grad: bfloat16 [12288, 4096], P('ctx', 'head')
- key_grad: bfloat16 [1536, 4096], P('ctx', 'head')
- value_grad: bfloat16 [1536, 4096], P('ctx', 'head')
All inputs are finite; a program needn't handle non-finite values.
Results may differ from a plain program's by a relative error of at most 0.0085.
Values may be sent and summed in bfloat16 or wider, within the bound.
No kernel may reach another device: no remote copies, remote signals or barrier semaphores. Data moves between devices by JAX's collectives and lax.ppermute only.
A program may use at most 64 MiB of HBM per device.

v0:
```python
import jax
import jax.numpy as jnp
from jax import lax
from jax.sharding import PartitionSpec as P

DH = 64


def local(queries, enc_keys, enc_values, grad_out, out_weight):
    query_rows, head_width = queries.shape
    heads_here = head_width // DH
    score_scale = DH ** (-0.5)
    head_grads = lax.dot_general(
        lax.all_gather(grad_out, "head", axis=1, tiled=True),
        out_weight,
        (((1,), (1,)), ((), ())),
        preferred_element_type=jnp.float32,
    ).astype(jnp.bfloat16)
    query_heads = queries.reshape(query_rows, heads_here, DH)
    grad_heads = head_grads.reshape(query_rows, heads_here, DH)

    def block_scores(key_block):
        key_count = key_block.shape[0]
        return score_scale * jnp.einsum(
            "qhd,khd->hqk",
            query_heads,
            key_block.reshape(key_count, heads_here, DH),
            preferred_element_type=jnp.float32,
        )

    def block_attention(row_stats, pieces):
        scores = block_scores(pieces[0])
        return jnp.exp(scores - row_stats[0][:, :, None]) / row_stats[1][:, :, None]

    row_top = jnp.full((heads_here, query_rows), -1e30, jnp.float32)
    scores = block_scores((lax.all_gather(enc_keys, "ctx", axis=0, tiled=True),)[0])
    new_top = jnp.maximum(row_top, jnp.max(scores, axis=2))
    exponent = jnp.exp(scores - new_top[:, :, None])
    row_stats = (new_top, jnp.sum(exponent, axis=2))
    pieces = (
        lax.all_gather(enc_keys, "ctx", axis=0, tiled=True),
        lax.all_gather(enc_values, "ctx", axis=0, tiled=True),
    )
    attention_low = block_attention(row_stats, pieces).astype(jnp.bfloat16)
    value_block = pieces[1].reshape(pieces[1].shape[0], heads_here, DH)
    attended = jnp.einsum(
        "hqk,khd->qhd", attention_low, value_block, preferred_element_type=jnp.float32
    )
    row_delta = jnp.einsum("qhd,qhd->hq", grad_heads.astype(jnp.float32), attended)
    pieces = (
        lax.all_gather(enc_keys, "ctx", axis=0, tiled=True),
        lax.all_gather(enc_values, "ctx", axis=0, tiled=True),
    )
    attention = block_attention(row_stats, pieces)
    value_block = pieces[1].reshape(pieces[1].shape[0], heads_here, DH)
    prob_grad = jnp.einsum(
        "qhd,khd->hqk", grad_heads, value_block, preferred_element_type=jnp.float32
    )
    score_grad = (score_scale * attention * (prob_grad - row_delta[:, :, None])).astype(
        jnp.bfloat16
    )
    attention_low, score_grad = (attention.astype(jnp.bfloat16), score_grad)
    key_count = pieces[0].shape[0]
    key_term = jnp.einsum(
        "hqk,qhd->khd", score_grad, query_heads, preferred_element_type=jnp.float32
    )
    value_term = jnp.einsum(
        "hqk,qhd->khd", attention_low, grad_heads, preferred_element_type=jnp.float32
    )
    key_term, value_term = (
        key_term.reshape(key_count, head_width),
        value_term.reshape(key_count, head_width),
    )
    key_block = pieces[0]
    key_heads = key_block.reshape(key_block.shape[0], heads_here, DH)
    query_sum = jnp.einsum(
        "hqk,khd->qhd", score_grad, key_heads, preferred_element_type=jnp.float32
    )
    key_grad, value_grad = (
        lax.psum_scatter(key_term, "ctx", scatter_dimension=0, tiled=True),
        lax.psum_scatter(value_term, "ctx", scatter_dimension=0, tiled=True),
    )
    query_grad = query_sum.reshape(query_rows, head_width).astype(jnp.bfloat16)
    return (query_grad, key_grad.astype(jnp.bfloat16), value_grad.astype(jnp.bfloat16))


def solution(mesh):
    return jax.shard_map(
        local,
        mesh=mesh,
        in_specs=(
            P("ctx", "head"),
            P("ctx", "head"),
            P("ctx", "head"),
            P("ctx", "head"),
            P("head", None),
        ),
        out_specs=(P("ctx", "head"), P("ctx", "head"), P("ctx", "head")),
        check_vma=False,
    )
```

profile of v0, /device:TPU:6, one launch (start us, length us, event | category | flops | bytes accessed | tf_op | source)
XLA Modules:
  0.0 771.3 jit_solution(18004836322919954678)
XLA Ops:
  7.2 0.0 copy-start
  7.2 0.0 all-gather.2.cloned.1.call-start
  7.2 0.7 all-gather.2.cloned.1.call-update
  7.9 0.0 reduce-scatter.3.cloned.1.call-start
  8.0 130.2 %all_gather.14 = bf16[1536,256]{1,0:T(8,128)(2,1)S(1)} all-gather(bf16[32,256]{1,0:T(8,128)(2,1)} %param.7), channel_id=1, replica_groups=mesh['ctx'=48,'head'=16] {'ctx'}, dimensions={0}, use_global_device_ids=true | all-gather | bytes 802816 | tf_op jit(solution)/shard_map/all_gather | solution.py:52
  138.1 1.2 copy.17
  139.4 1.0 copy.15
  140.4 120.7 %all_gather.12 = bf16[1536,256]{1,0:T(8,128)(2,1)} all-gather(bf16[32,256]{1,0:T(8,128)(2,1)} %param.6), channel_id=1, replica_groups=mesh['ctx'=48,'head'=16] {'ctx'}, dimensions={0}, use_global_device_ids=true | all-gather | bytes 802816 | tf_op jit(solution)/shard_map/all_gather | solution.py:51
  261.1 1.4 copy.16
  262.5 1.1 multiply_reduce_fusion
  263.6 0.0 copy-start.1
  263.6 2.6 copy-done.1
  266.3 1.2 fusion.1
  267.4 0.0 all-gather.2.cloned.1.call-done
  267.5 0.0 copy-done
  267.5 3.0 convolution_convert_fusion.1
  270.5 1.0 copy.26
  271.5 0.0 copy-start.3
  271.5 0.0 copy-start.4
  271.5 4.5 fusion.9
  276.0 0.0 copy-done.3
  276.0 0.0 copy-done.4
  276.0 4.2 multiply_convert_fusion
  280.3 0.0 copy-start.2
  280.3 1.7 copy-done.2
  282.0 0.0 copy-start.5
  282.0 1.8 fusion.14
  283.8 3.1 copy.18
  286.8 0.0 reduce-scatter.3.cloned.1.call-update
  286.8 0.0 reduce-scatter.5.cloned.1.call-start
  286.9 0.0 copy-done.5
  286.9 5.4 fusion.2
  292.3 3.0 copy.19
  295.4 0.0 reduce-scatter.5.cloned.1.call-update
  295.4 3.0 convolution_convert_fusion
  298.4 0.8 copy.20
  299.1 223.8 %reduce-scatter.3.cloned.1.call-done = f32[32,256]{1,0:T(8,128)} async-done(((f32[1536,256]{1,0:T(8,128)}), f32[32,256]{1,0:T(8,128)}) %reduce-scatter.3.cloned.1.call-update) | async-done | bytes 32784 | tf_op jit(solution)/shard_map/reduce_scatter | solution.py:80
  522.9 1.4 convert_element_type.32
  524.3 239.1 %reduce-scatter.5.cloned.1.call-done = f32[32,256]{1,0:T(8,128)} async-done(((f32[1536,256]{1,0:T(8,128)}), f32[32,256]{1,0:T(8,128)}) %reduce-scatter.5.cloned.1.call-update) | async-done | bytes 32784 | tf_op jit(solution)/shard_map/reduce_scatter | solution.py:81
  763.4 1.4 convert_element_type.33
  (1 shorter events, 0.0 us)
Async XLA Ops:
  7.2 260.3 %copy-start = (bf16[256,4096]{1,0:T(8,128)(2,1)S(1)}, bf16[256,4096]{1,0:T(8,128)(2,1)}, u32[]{:S(2)}) copy-start(bf16[256,4096]{1,0:T(8,128)(2,1)} %param.9) | copy-start | bytes 6291460
  7.2 260.3 %all-gather.2.cloned.1.call-start = ((), (), s32[]{:S(2)}) async-start(), calls=%async_computation.2 | async-start | bytes 2228224 | tf_op jit(solution)/shard_map/all_gather | solution.py:14
  7.9 515.0 %reduce-scatter.3.cloned.1.call-start = ((), (), s32[]{:S(2)}) async-start(), calls=%async_computation.3 | async-start | bytes 1605632 | tf_op jit(solution)/shard_map/reduce_scatter | solution.py:80
  263.6 2.7 copy-start.1
  271.5 4.5 copy-start.3
  271.5 4.5 copy-start.4
  280.3 1.7 copy-start.2
  282.0 4.9 copy-start.5
  286.8 476.5 %reduce-scatter.5.cloned.1.call-start = ((), (), s32[]{:S(2)}) async-start(), calls=%async_computation.4 | async-start | bytes 1605632 | tf_op jit(solution)/shard_map/reduce_scatter | solution.py:81
Sparse Core Ops, SparseCore 0:
  11.7 79.7 all-gather.1
  287.0 235.8 reduce-scatter.2
  526.0 237.3 reduce-scatter.4
where the time goes:
time: 772 us; the launch traced here: 771 us
  waiting for transfers between devices  464 us (60%)
  blocking collectives  251 us (33%)
  matrix products  23 us (3%)
  local copies, waits for them, and re-layouts  15.9 us (2%)
  between operations  13.9 us (2%)
    reduce_scatter x1, waiting for transfers between devices, local(): lax.psum_scatter(value_term, 'ctx', scatter_dimension=0, tiled=True)  239 us
    reduce_scatter x1, waiting for transfers between devices, local(): lax.psum_scatter(key_term, 'ctx', scatter_dimension=0, tiled=True)  224 us
    all_gather x1, blocking collectives, local(): lax.all_gather(enc_values, 'ctx', axis=0, tiled=True)  130 us
    all_gather x1, blocking collectives, local(): lax.all_gather(enc_keys, 'ctx', axis=0, tiled=True)  121 us
  transfers between devices with their start and end apart: 3, of which 2 were waited for; matrix products, arithmetic and copies ran while one was open for 3% of the time, Pallas kernels for 0%

commit v1 on v0

v1 whole, which is shorter than its diff:
```python
import jax
import jax.numpy as jnp
from jax import lax
from jax.sharding import Mesh, PartitionSpec as P

DH = 64
BF = jnp.bfloat16
F32 = jnp.float32
Z, YL, YH, X, C = 12, 4, 2, 4, 2
CTX = ("z", "yl")
HEAD = ("yh", "x", "c")


def pack(block):
    rows = block.shape[0]
    return (
        block.reshape(2, rows // 2, YL, DH).transpose(2, 1, 0, 3).reshape(YL, rows // 2, 2 * DH)
    )


def unpack_rows(packed):
    n, half, _ = packed.shape
    return packed.reshape(n, half, 2, DH).transpose(0, 2, 1, 3).reshape(n * half * 2, DH)


def pack_rows(rows):
    half = rows.shape[0] // YL // 2
    return rows.reshape(YL, 2, half, DH).transpose(0, 2, 1, 3).reshape(YL, half, 2 * DH)


def unpack(packed):
    n, half, _ = packed.shape
    return packed.reshape(n, half, 2, DH).transpose(2, 1, 0, 3).reshape(2 * half, n * DH)


def exchange(block, axis):
    return lax.all_to_all(block, axis, 0, 0, tiled=True)


def local(queries, enc_keys, enc_values, grad_out, out_weight):
    rows, width = queries.shape
    keys_here = enc_keys.shape[0]
    key_count = keys_here * Z * YL
    other = lax.ppermute(grad_out, "yh", [(0, 1), (1, 0)])
    mine = lax.axis_index("yh")
    both = jnp.where(mine == 0, jnp.stack([grad_out, other]), jnp.stack([other, grad_out]))
    over_x = exchange(jnp.broadcast_to(both[None], (X,) + both.shape), "x")
    over_c = lax.ppermute(over_x, "c", [(0, 1), (1, 0)])
    core = lax.axis_index("c")
    weight = out_weight.reshape(width, YH, X, C, width)
    w_mine = lax.dynamic_index_in_dim(weight, core, 3, keepdims=False)
    w_other = lax.dynamic_index_in_dim(weight, 1 - core, 3, keepdims=False)
    head_grads = (
        jnp.einsum("xyrd,wyxd->rw", over_x, w_mine, preferred_element_type=F32)
        + jnp.einsum("xyrd,wyxd->rw", over_c, w_other, preferred_element_type=F32)
    ).astype(BF)

    q_packed = exchange(pack(queries), "yl")
    kv = jnp.concatenate(
        [enc_keys.reshape(keys_here, YL, DH), enc_values.reshape(keys_here, YL, DH)], axis=2
    ).transpose(1, 0, 2)
    kv_all = exchange(
        jnp.broadcast_to(kv[None], (Z,) + kv.shape).reshape(Z * YL, keys_here, 2 * DH), CTX
    ).reshape(key_count, 2 * DH)
    g_packed = exchange(pack(head_grads), "yl")

    q = unpack_rows(q_packed)
    g = unpack_rows(g_packed)
    k, v = kv_all[:, :DH], kv_all[:, DH:]
    scale = DH ** (-0.5)
    scores = scale * jnp.dot(q, k.T, preferred_element_type=F32)
    top = jnp.max(scores, axis=1, keepdims=True)
    exponent = jnp.exp(scores - top)
    attention = exponent / jnp.sum(exponent, axis=1, keepdims=True)
    low = attention.astype(BF)
    attended = jnp.dot(low, v, preferred_element_type=F32)
    delta = jnp.sum(g.astype(F32) * attended, axis=1, keepdims=True)
    prob_grad = jnp.dot(g, v.T, preferred_element_type=F32)
    score_grad = (scale * attention * (prob_grad - delta)).astype(BF)
    dq = jnp.dot(score_grad, k, preferred_element_type=F32).astype(BF)
    dk = jnp.dot(score_grad.T, q, preferred_element_type=F32)
    dv = jnp.dot(low.T, g, preferred_element_type=F32)
    dkv = jnp.concatenate([dk, dv], axis=1).astype(BF)

    dkv_parts = exchange(dkv.reshape(Z * YL, keys_here, 2 * DH), CTX)
    dkv_sum = jnp.sum(dkv_parts.reshape(Z, YL, keys_here, 2 * DH).astype(F32), axis=0).astype(BF)
    query_grad = unpack(exchange(pack_rows(dq), "yl"))
    heads_last = dkv_sum.transpose(1, 0, 2)
    key_grad = heads_last[:, :, :DH].reshape(keys_here, width)
    value_grad = heads_last[:, :, DH:].reshape(keys_here, width)
    return query_grad, key_grad, value_grad


def solution(mesh):
    fine = Mesh(mesh.devices.reshape(Z, YL, YH, X, C), CTX + HEAD)
    both = P(CTX, HEAD)
    return jax.shard_map(
        local,
        mesh=fine,
        in_specs=(both, both, both, both, P(HEAD, None)),
        out_specs=(both, both, both),
        check_vma=False,
    )
```

time: 772 us -> 152 us (0.20)
  waiting for transfers between devices: 464 us -> 37.1 us
  blocking collectives: 251 us -> 0 us
  starting transfers between devices: 0.12 us -> 55 us
  local copies, waits for them, and re-layouts: 15.9 us -> 29.9 us
  between operations: 13.9 us -> 0.89 us
    reduce_scatter x2 -> x0, waiting for transfers between devices: 463 us -> none  [the longest x1 239 us: local(): lax.psum_scatter(value_term, 'ctx', scatter_dimension=0, tiled=True)]
    all_gather x2 -> x0, blocking collectives: 251 us -> none  [the longest x1 130 us: local(): lax.all_gather(enc_values, 'ctx', axis=0, tiled=True)]
    all_to_all x0 -> x6, starting transfers between devices: none -> 45.4 us  [exchange(): return lax.all_to_all(block, axis, 0, 0, tiled=True)]
    all_to_all x0 -> x6, waiting for transfers between devices: none -> 37.1 us  [exchange(): return lax.all_to_all(block, axis, 0, 0, tiled=True)]
    ppermute x0 -> x2, starting transfers between devices: none -> 9.66 us  [the longest x1 7.74 us: local(): other = lax.ppermute(grad_out, 'yh', [(0, 1), (1, 0)])]
    dot_general x7 -> x8, matrix products: 23 us -> 19.3 us  [the longest x1 5.77 us: local(): prob_grad = jnp.dot(g, v.T, preferred_element_type=F32)]
  transfers between devices with their start and end apart: 3 -> 8, of which waited for: 2 -> 6; matrix products, arithmetic and copies ran while one was open for 3% -> 21% of each run, Pallas kernels for 0% -> 0%
where the time goes in v1:
time: 152 us; the launch traced here: 149 us
  starting transfers between devices  55 us (36%)
  waiting for transfers between devices  37.1 us (24%)
  local copies, waits for them, and re-layouts  29.9 us (20%)
  matrix products  19.3 us (13%)
  other arithmetic  7.17 us (5%)
    all_to_all x6, starting transfers between devices, exchange(): return lax.all_to_all(block, axis, 0, 0, tiled=True)  45.4 us
    all_to_all x6, waiting for transfers between devices, exchange(): return lax.all_to_all(block, axis, 0, 0, tiled=True)  37.1 us
    ppermute x1, starting transfers between devices, local(): other = lax.ppermute(grad_out, 'yh', [(0, 1), (1, 0)])  7.74 us
    dynamic_slice x1, local copies, waits for them, and re-layouts, local(): w_other = lax.dynamic_index_in_dim(weight, 1 - core, 3, keepdims=False)  6.31 us
    unnamed x17, local copies, waits for them, and re-layouts  6.29 us
    dot_general x1, matrix products, local(): prob_grad = jnp.dot(g, v.T, preferred_element_type=F32)  5.77 us
    reshape x4, local copies, waits for them, and re-layouts, unpack_rows(): packed.reshape(n, half, 2, DH).transpose(0, 2, 1, 3)  4.03 us
    convert_element_type x1, other arithmetic, local(): low = attention.astype(BF)  3.95 us
  transfers between devices with their start and end apart: 8, of which 6 were waited for; matrix products, arithmetic and copies ran while one was open for 21% of the time, Pallas kernels for 0%

profile of v1, /device:TPU:6, one launch (start us, length us, event | category | flops | bytes accessed | tf_op | source)
XLA Modules:
  0.0 149.5 jit_solution(1207970986292156247)
XLA Ops:
  0.6 7.7 %collective-permute-start = (bf16[256,256]{1,0:T(8,128)(2,1)}, bf16[256,256]{1,0:T(8,128)(2,1)S(1)}, u32[]{:S(2)}, u32[]{:S(2)}) collective-permute-start(bf16[256,256]{1,0:T(8,128)(2,1)} %param.8), channel_id=1, source_target_pairs={{0,8},{8,0},{1,9},{9,1},{2,10},{10,2},{3,11},{11,3},{4,12},{12,4},... | collective-permute-start | bytes 393224 | tf_op jit(solution)/shard_map/ppermute | solution.py:44
  8.4 1.0 copy.39
  9.4 0.7 copy.40
  10.1 3.3 %all-to-all-start.1 = ((bf16[4,128,128]{1,2,0:T(8,128)(2,1)}), bf16[4,128,128]{1,2,0:T(8,128)(2,1)S(1)}, u32[]{:S(2)}, u32[]{:S(2)}) async-start(bf16[4,128,128]{1,2,0:T(8,128)(2,1)} %bitcast.4), calls=%async_computation.1 | async-start | bytes 262144 | tf_op jit(solution)/shard_map/all_to_all | solution.py:37
  13.4 1.0 maximum_select_fusion
  14.5 5.0 %all-to-all-done.1 = bf16[4,128,128]{1,2,0:T(8,128)(2,1)S(1)} async-done(((bf16[4,128,128]{1,2,0:T(8,128)(2,1)}), bf16[4,128,128]{1,2,0:T(8,128)(2,1)S(1)}, u32[]{:S(2)}, u32[]{:S(2)}) %all-to-all-start.1) | async-done | bytes 131104 | tf_op jit(solution)/shard_map/all_to_all | solution.py:37
  19.5 1.0 broadcast_in_dim.5
  20.5 7.0 %all-to-all-start.2 = ((bf16[4,2,256,256]{3,2,1,0:T(8,128)(2,1)}), bf16[4,2,256,256]{3,2,1,0:T(8,128)(2,1)S(1)}, u32[]{:S(2)}, u32[]{:S(2)}) async-start(bf16[4,2,256,256]{3,2,1,0:T(8,128)(2,1)} %broadcast_in_dim.5), calls=%async_computation.2 | async-start | bytes 2097152 | tf_op jit(solution)/shard_map/all_to_all | solution.py:37
  27.5 0.8 reshape.108
  28.3 0.8 reshape.109
  29.2 7.5 %all-to-all-done.2 = bf16[4,2,256,256]{3,2,1,0:T(8,128)(2,1)S(1)} async-done(((bf16[4,2,256,256]{3,2,1,0:T(8,128)(2,1)}), bf16[4,2,256,256]{3,2,1,0:T(8,128)(2,1)S(1)}, u32[]{:S(2)}, u32[]{:S(2)}) %all-to-all-start.2) | async-done | bytes 1048608 | tf_op jit(solution)/shard_map/all_to_all | solution.py:37
  36.7 0.8 broadcast_in_dim.4
  37.6 17.9 %all-to-all-start = ((bf16[48,32,128]{2,1,0:T(8,128)(2,1)}), bf16[48,32,128]{2,1,0:T(8,128)(2,1)S(1)}, u32[]{:S(2)}, u32[]{:S(2)}) async-start(bf16[48,32,128]{2,1,0:T(8,128)(2,1)} %bitcast.1), calls=%async_computation | async-start | bytes 786432 | tf_op jit(solution)/shard_map/all_to_all | solution.py:37
  55.5 3.3 %reshape.116 = bf16[256,2,4,2,256]{4,3,2,1,0:T(2,128)(2,1)S(1)} reshape(bf16[256,4096]{1,0:T(8,128)(2,1)} %param.9) | data formatting | bytes 4194304 | tf_op jit(solution)/shard_map/reshape | solution.py:50
  58.8 6.3 %constant_dynamic-slice_fusion = (bf16[256,2,4,1,256]{4,3,2,1,0:T(2,128)(2,1)}, bf16[256,2,4,1,256]{4,3,2,1,0:T(2,128)(2,1)}) fusion(bf16[256,2,4,2,256]{4,3,2,1,0:T(2,128)(2,1)S(1)} %reshape.116, s32[]{:T(128)S(6)} %select_n.22, s32[]{:T(128)S(6)} %select_n.21), kind=kLoop, calls=%fused_computation.29 | loop fusion | bytes 4194312 | tf_op jit(solution)/shard_map/jit(dynamic_index_in_dim)/dynamic_slice | solution.py:52
  65.1 0.1 copy.41
  65.3 0.7 reshape.130
  66.1 1.9 %collective-permute-start.1 = (bf16[4,2,256,256]{3,2,1,0:T(8,128)(2,1)S(1)}, bf16[4,2,256,256]{3,2,1,0:T(8,128)(2,1)S(1)}, u32[]{:S(2)}, u32[]{:S(2)}) collective-permute-start(bf16[4,2,256,256]{3,2,1,0:T(8,128)(2,1)S(1)} %all-to-all-done.2), channel_id=1, source_target_pairs={{0,1},{1,0},{2,3},{3,2},{4,5},{5,4},{6,7},{7,6},{8,9},{9,8},{10,11... | collective-permute-start | bytes 3145736 | tf_op jit(solution)/shard_map/ppermute | solution.py:48
  68.0 2.4 %convolution_bitcast_fusion.1 = f32[256,256]{1,0:T(8,128)S(1)} fusion(bf16[4,2,256,256]{3,2,1,0:T(8,128)(2,1)S(1)} %all-to-all-done.2, bf16[256,2,4,1,256]{4,3,2,1,0:T(2,128)(2,1)} %get-tuple-element.13), kind=kOutput, calls=%fused_computation.13 | convolution fusion | flops 268435456 | bytes 2359296 | tf_op jit(solution)/shard_map/xyrd,wyxd->rw/dot_general | solution.py:54
  70.4 4.5 %all-to-all-done = bf16[48,32,128]{2,1,0:T(8,128)(2,1)S(1)} async-done(((bf16[48,32,128]{2,1,0:T(8,128)(2,1)}), bf16[48,32,128]{2,1,0:T(8,128)(2,1)S(1)}, u32[]{:S(2)}, u32[]{:S(2)}) %all-to-all-start) | async-done | bytes 393248 | tf_op jit(solution)/shard_map/all_to_all | solution.py:37
  74.9 1.0 multiply_reduce_fusion
  75.9 2.6 %copy-done = f32[1536,1024]{1,0:T(8,128)} copy-done((f32[1536,1024]{1,0:T(8,128)}, f32[1536,1024]{1,0:T(8,128)S(1)}, u32[]{:S(2)}) %copy-start) | copy-done | bytes 6291480
  78.6 1.1 fusion.3
  79.6 0.8 fusion.7
  80.6 0.7 copy.45
  81.3 4.1 %all-to-all-start.3 = ((bf16[4,128,128]{1,2,0:T(8,128)(2,1)}), bf16[4,128,128]{1,2,0:T(8,128)(2,1)}, u32[]{:S(2)}, u32[]{:S(2)}) async-start(bf16[4,128,128]{1,2,0:T(8,128)(2,1)} %bitcast.17), calls=%async_computation.3 | async-start | bytes 262144 | tf_op jit(solution)/shard_map/all_to_all | solution.py:37
  85.4 4.0 %fusion.20 = bf16[1536,1024]{1,0:T(8,128)(2,1)S(1)} fusion(f32[1024]{0:T(1024)S(1)} %fusion.3, f32[1024]{0:T(1024)S(1)} %get-tuple-element.16, f32[1536,1024]{1,0:T(8,128)} %copy-done), kind=kLoop, calls=%fused_computation.32 | loop fusion | flops 6291456 | bytes 9445376 | tf_op jit(solution)/shard_map/convert_element_type | solution.py:75
  89.3 1.8 %all-to-all-done.3 = bf16[4,128,128]{1,2,0:T(8,128)(2,1)} async-done(((bf16[4,128,128]{1,2,0:T(8,128)(2,1)}), bf16[4,128,128]{1,2,0:T(8,128)(2,1)}, u32[]{:S(2)}, u32[]{:S(2)}) %all-to-all-start.3) | async-done | bytes 131104 | tf_op jit(solution)/shard_map/all_to_all | solution.py:37
  91.2 1.7 %copy.46 = bf16[4,2,128,64]{2,1,0,3:T(2,128)(2,1)} copy(bf16[4,2,128,64]{2,3,1,0:T(8,128)(2,1)} %bitcast.19) | data formatting | bytes 262144 | tf_op jit(solution)/shard_map/transpose | solution.py:23
  92.9 1.6 %reshape.120 = bf16[1024,64]{0,1:T(8,128)(2,1)} reshape(bf16[4,2,128,64]{2,1,0,3:T(2,128)(2,1)} %copy.46) | data formatting | bytes 262144 | tf_op jit(solution)/shard_map/reshape | solution.py:23
  94.5 1.6 %reshape.131 = bf16[1024,64,1]{0,1,2:T(8,128)(2,1)} reshape(bf16[4,2,128,64]{2,1,0,3:T(2,128)(2,1)} %copy.46) | data formatting | bytes 262144 | tf_op jit(solution)/shard_map/reshape | solution.py:23
  96.1 1.9 %fusion.11 = f32[1024]{0:T(1024)S(1)} fusion(bf16[1536,1024]{1,0:T(8,128)(2,1)S(1)} %fusion.20, bf16[1536,128]{1,0:T(8,128)(2,1)S(1)} %bitcast.82, bf16[1024,64]{0,1:T(8,128)(2,1)} %reshape.120), kind=kOutput, calls=%fused_computation.17 | convolution fusion | flops 201522176 | bytes 3674112 | tf_op jit(solution)/shard_map/dot_general | solution.py:76
  98.0 5.8 %fusion = (bf16[1536,1024]{1,0:T(8,128)(2,1)}, f32[1024,1536]{0,1:T(8,128)S(1)}) fusion(f32[1024]{0:T(1024)S(1)} %fusion.11, f32[1024]{0:T(1024)S(1)} %fusion.3, f32[1024]{0:T(1024)S(1)} %get-tuple-element.16, f32[1536,1024]{1,0:T(8,128)} %copy-done, bf16[1024,64]{0,1:T(8,128)(2,1)} %reshape.120, bf16[1536,128]{1,0:T(8,128)(2,1)S(1)} %bitcast.83), kind=kOutput, calls=%fused_computation.1 | convolution fusion | flops 212336640 | bytes 16265216 | tf_op jit(solution)/shard_map/dot_general | solution.py:78
  103.8 2.8 %fusion.8 = bf16[1024,64]{0,1:T(8,128)(2,1)} fusion(f32[1024,1536]{0,1:T(8,128)S(1)} %get-tuple-element.19, f32[1024]{0:T(1024)S(1)} %fusion.11, bf16[1536,128]{1,0:T(8,128)(2,1)S(1)} %bitcast.84, f32[1536,1024]{1,0:T(8,128)S(1)} %bitcast.79, f32[1024]{0:T(1024)S(1)} %fusion.3, f32[1024]{0:T(1024)S(1)} %get-tuple-element.16), kind=kOutput, calls=%fused_computation.16 | convolution fusion | flops 212402176 | bytes 13119488 | tf_op jit(solution)/shard_map/dot_general | solution.py:80
  106.6 1.0 reshape.121
  107.6 0.7 copy.48
  108.3 3.3 %all-to-all-start.4 = ((bf16[4,128,128]{1,2,0:T(8,128)(2,1)}), bf16[4,128,128]{1,2,0:T(8,128)(2,1)S(1)}, u32[]{:S(2)}, u32[]{:S(2)}) async-start(bf16[4,128,128]{1,2,0:T(8,128)(2,1)} %bitcast.21), calls=%async_computation.4 | async-start | bytes 262144 | tf_op jit(solution)/shard_map/all_to_all | solution.py:37
  111.6 1.9 %convolution_convert_fusion = bf16[48,32,64]{2,1,0:T(8,128)(2,1)S(1)} fusion(bf16[48,32,1024]{2,1,0:T(8,128)(2,1)S(1)} %bitcast.80, bf16[1024,64,1]{0,1,2:T(8,128)(2,1)} %reshape.131), kind=kOutput, calls=%fused_computation.9 | convolution fusion | flops 201424896 | bytes 3473408 | tf_op jit(solution)/shard_map/dot_general | solution.py:82
  113.5 2.9 %convolution_convert_fusion.1 = bf16[48,32,64]{2,1,0:T(8,128)(2,1)S(1)} fusion(bf16[48,32,1024]{2,1,0:T(8,128)(2,1)} %bitcast.93, bf16[1024,64,1]{0,1,2:T(8,128)(2,1)} %reshape.130), kind=kOutput, calls=%fused_computation.10 | convolution fusion | flops 201424896 | bytes 3473408 | tf_op jit(solution)/shard_map/dot_general | solution.py:81
  116.3 1.0 pad_maximum_fusion
  117.3 0.2 all-to-all-done.4
  117.5 0.7 copy-done.2
  118.1 9.7 %all-to-all-start.5 = ((bf16[48,32,128]{2,1,0:T(8,128)(2,1)}), bf16[48,32,128]{2,1,0:T(8,128)(2,1)S(1)}, u32[]{:S(2)}, u32[]{:S(2)}) async-start(bf16[48,32,128]{2,1,0:T(8,128)(2,1)} %pad_maximum_fusion), calls=%async_computation.5 | async-start | bytes 786432 | tf_op jit(solution)/shard_map/all_to_all | solution.py:37
  127.9 1.1 copy.56
  129.0 0.9 reshape.132
  129.8 18.0 %all-to-all-done.5 = bf16[48,32,128]{2,1,0:T(8,128)(2,1)S(1)} async-done(((bf16[48,32,128]{2,1,0:T(8,128)(2,1)}), bf16[48,32,128]{2,1,0:T(8,128)(2,1)S(1)}, u32[]{:S(2)}, u32[]{:S(2)}) %all-to-all-start.5) | async-done | bytes 393248 | tf_op jit(solution)/shard_map/all_to_all | solution.py:37
  148.0 0.7 reshape.127
  148.8 0.7 reshape.126
  (25 shorter events, 0.6 us)
Async XLA Ops:
  0.6 12.8 %collective-permute-start = (bf16[256,256]{1,0:T(8,128)(2,1)}, bf16[256,256]{1,0:T(8,128)(2,1)S(1)}, u32[]{:S(2)}, u32[]{:S(2)}) collective-permute-start(bf16[256,256]{1,0:T(8,128)(2,1)} %param.8), channel_id=1, source_target_pairs={{0,8},{8,0},{1,9},{9,1},{2,10},{10,2},{3,11},{11,3},{4,12},{12,4},... | collective-permute-start | bytes 393224 | tf_op jit(solution)/shard_map/ppermute | solution.py:44
  10.1 9.4 %all-to-all-start.1 = ((bf16[4,128,128]{1,2,0:T(8,128)(2,1)}), bf16[4,128,128]{1,2,0:T(8,128)(2,1)S(1)}, u32[]{:S(2)}, u32[]{:S(2)}) async-start(bf16[4,128,128]{1,2,0:T(8,128)(2,1)} %bitcast.4), calls=%async_computation.1 | async-start | bytes 262144 | tf_op jit(solution)/shard_map/all_to_all | solution.py:37
  19.5 18.1 %copy-start.3 = (bf16[4,128,128]{1,2,0:T(8,128)(2,1)}, bf16[4,128,128]{1,2,0:T(8,128)(2,1)S(1)}, u32[]{:S(2)}) copy-start(bf16[4,128,128]{1,2,0:T(8,128)(2,1)S(1)} %all-to-all-done.1) | copy-start | bytes 393220
  20.5 16.2 %all-to-all-start.2 = ((bf16[4,2,256,256]{3,2,1,0:T(8,128)(2,1)}), bf16[4,2,256,256]{3,2,1,0:T(8,128)(2,1)S(1)}, u32[]{:S(2)}, u32[]{:S(2)}) async-start(bf16[4,2,256,256]{3,2,1,0:T(8,128)(2,1)} %broadcast_in_dim.5), calls=%async_computation.2 | async-start | bytes 2097152 | tf_op jit(solution)/shard_map/all_to_all | solution.py:37
  37.6 37.4 %all-to-all-start = ((bf16[48,32,128]{2,1,0:T(8,128)(2,1)}), bf16[48,32,128]{2,1,0:T(8,128)(2,1)S(1)}, u32[]{:S(2)}, u32[]{:S(2)}) async-start(bf16[48,32,128]{2,1,0:T(8,128)(2,1)} %bitcast.1), calls=%async_computation | async-start | bytes 786432 | tf_op jit(solution)/shard_map/all_to_all | solution.py:37
  58.8 6.3 %copy-start.4 = (bf16[4,128,128]{1,2,0:T(8,128)(2,1)S(1)}, bf16[4,128,128]{1,2,0:T(8,128)(2,1)}, u32[]{:S(2)}) copy-start(bf16[4,128,128]{1,2,0:T(8,128)(2,1)} %copy-done.3) | copy-start | bytes 393220
  66.1 13.6 %collective-permute-start.1 = (bf16[4,2,256,256]{3,2,1,0:T(8,128)(2,1)S(1)}, bf16[4,2,256,256]{3,2,1,0:T(8,128)(2,1)S(1)}, u32[]{:S(2)}, u32[]{:S(2)}) collective-permute-start(bf16[4,2,256,256]{3,2,1,0:T(8,128)(2,1)S(1)} %all-to-all-done.2), channel_id=1, source_target_pairs={{0,1},{1,0},{2,3},{3,2},{4,5},{5,4},{6,7},{7,6},{8,9},{9,8},{10,11... | collective-permute-start | bytes 3145736 | tf_op jit(solution)/shard_map/ppermute | solution.py:48
  74.9 4.7 %copy-start.1 = (bf16[256,2,4,1,256]{4,3,2,1,0:T(2,128)(2,1)S(1)}, bf16[256,2,4,1,256]{4,3,2,1,0:T(2,128)(2,1)}, u32[]{:S(2)}) copy-start(bf16[256,2,4,1,256]{4,3,2,1,0:T(2,128)(2,1)} %get-tuple-element.12) | copy-start | bytes 3145732
  75.9 2.7 %copy-start = (f32[1536,1024]{1,0:T(8,128)}, f32[1536,1024]{1,0:T(8,128)S(1)}, u32[]{:S(2)}) copy-start(f32[1536,1024]{1,0:T(8,128)S(1)} %get-tuple-element.17) | copy-start | bytes 18874372
  81.3 9.9 %all-to-all-start.3 = ((bf16[4,128,128]{1,2,0:T(8,128)(2,1)}), bf16[4,128,128]{1,2,0:T(8,128)(2,1)}, u32[]{:S(2)}, u32[]{:S(2)}) async-start(bf16[4,128,128]{1,2,0:T(8,128)(2,1)} %bitcast.17), calls=%async_computation.3 | async-start | bytes 262144 | tf_op jit(solution)/shard_map/all_to_all | solution.py:37
  96.1 7.7 %slice-start = ((s8[6291456]{0:T(1024)(128)(4,1)}), s8[4194304]{0:T(1024)(128)(4,1)S(1)}, s32[]{:S(2)}) async-start(s8[6291456]{0:T(1024)(128)(4,1)} %bitcast.78), calls=%async_computation.6 | async-start | bytes 8388608
  98.0 5.8 %slice-start.1 = ((s8[6291456]{0:T(1024)(128)(4,1)}), s8[2097152]{0:T(1024)(128)(4,1)S(1)}, s32[]{:S(2)}) async-start(s8[6291456]{0:T(1024)(128)(4,1)} %bitcast.78), calls=%async_computation.7 | async-start | bytes 4194304
  108.3 9.2 %all-to-all-start.4 = ((bf16[4,128,128]{1,2,0:T(8,128)(2,1)}), bf16[4,128,128]{1,2,0:T(8,128)(2,1)S(1)}, u32[]{:S(2)}, u32[]{:S(2)}) async-start(bf16[4,128,128]{1,2,0:T(8,128)(2,1)} %bitcast.21), calls=%async_computation.4 | async-start | bytes 262144 | tf_op jit(solution)/shard_map/all_to_all | solution.py:37
  117.5 0.7 copy-start.2
  118.1 29.7 %all-to-all-start.5 = ((bf16[48,32,128]{2,1,0:T(8,128)(2,1)}), bf16[48,32,128]{2,1,0:T(8,128)(2,1)S(1)}, u32[]{:S(2)}, u32[]{:S(2)}) async-start(bf16[48,32,128]{2,1,0:T(8,128)(2,1)} %pad_maximum_fusion), calls=%async_computation.5 | async-start | bytes 786432 | tf_op jit(solution)/shard_map/all_to_all | solution.py:37
